TPU v7x, 32 devices: a whole 2x2x4 slice. The times are simulated.
32 devices in a mesh: band: 8 (over z, x), slab: 4 (over y, core).
Axes of the slice: x: 2, y: 2, z: 4, core: 2. Of those that a mesh axis runs over, the one named last changes fastest.
Arguments:
- orbitals: float32 [32, 48, 2304], P('band', 'slab'), may hold values from -6 to 6
- partners: int32 [8, 2], replicated, may hold values from 0 to 7, as said below
- counts: int32 [8, 2], replicated, may hold values from 1 to 4
Outputs:
- forces: float32 [32, 48, 2304], P('band', 'slab')
- energy: float32 [], replicated
Inputs may be any that keep to these rules, and one draw needn't show every extreme that they name: `partners`: row g names two different band groups, neither of them g.
All inputs are finite; a program needn't handle non-finite values.
Results may differ from a plain program's by a relative error of at most 0.0001.
Values sent between devices are 32-bit elements; how exact they have to be, the bound alone decides.
No kernel may reach another device: no remote copies, remote signals or barrier semaphores. Data moves between devices by JAX's collectives and lax.ppermute only.
A program may use at most 64 MiB of HBM per device.

v0:
```python
import math

import jax
import jax.numpy as jnp
from jax import lax
from jax.sharding import PartitionSpec as P

NX = 48
NY = 48
NZ = 48
NZP = 96


slater_coeff = -((3.0 / math.pi) ** (1.0 / 3.0))
exchange_mix = 0.25
screening = 0.25
highest = lax.Precision.HIGHEST


def dft_block(count_in, count_out, length, sign):
    row_iota = lax.broadcasted_iota(jnp.int32, (count_in, count_out), 0)
    col_iota = lax.broadcasted_iota(jnp.int32, (count_in, count_out), 1)
    phase_angle = 2.0 * math.pi / length * (row_iota * col_iota % length).astype(jnp.float32)
    cosine = jnp.cos(phase_angle)
    sine = jnp.sin(phase_angle)
    upper = jnp.stack([cosine, -sign * sine])
    lower = jnp.stack([sign * sine, cosine])
    return jnp.stack([upper, lower])


def wavenumber_sq(length):
    position = jnp.arange(length, dtype=jnp.int32)
    signed = jnp.where(position > length // 2, position - length, position).astype(jnp.float32)
    wave_number = 2.0 * math.pi / length * signed
    return wave_number * wave_number


def screened_potential(fields):
    spectrum = jnp.einsum(
        "coxyz,cdzk->doxyk", fields, dft_block(NZ, NZP, NZP, 1.0), precision=highest
    )
    spectrum = jnp.einsum(
        "coxyk,cdyq->doxqk", spectrum, dft_block(NY, NY, NY, 1.0), precision=highest
    )
    spectrum = jnp.einsum(
        "coxqk,cdxp->dopqk", spectrum, dft_block(NX, NX, NX, 1.0), precision=highest
    )
    total = (
        wavenumber_sq(NX)[:, None, None]
        + wavenumber_sq(NY)[None, :, None]
        + wavenumber_sq(NZP)[None, None, :]
    )
    kernel_table = 4.0 * math.pi / (NX * NY * NZP) / (total + screening * screening)
    spectrum = spectrum * kernel_table
    spectrum = jnp.einsum(
        "copqk,cdpx->doxqk", spectrum, dft_block(NX, NX, NX, -1.0), precision=highest
    )
    spectrum = jnp.einsum(
        "coxqk,cdqy->doxyk", spectrum, dft_block(NY, NY, NY, -1.0), precision=highest
    )
    return jnp.einsum(
        "coxyk,cdkz->doxyz", spectrum, dft_block(NZP, NZ, NZP, -1.0), precision=highest
    )


def pair_terms(own_orbs, visitors, active):
    per_device = own_orbs.shape[0]
    pair_density = own_orbs[None] * visitors * active[:, :, None, None]
    shaped = pair_density.reshape(2, per_device, NX, NY, NZ)
    fields = screened_potential(shaped).reshape(pair_density.shape)
    own_force = -exchange_mix * jnp.sum(fields * visitors, axis=0)
    partner_force = -exchange_mix * fields * own_orbs[None]
    energy_term = jnp.sum(pair_density * fields)
    return (own_force, partner_force, energy_term)


def request_rows(held_rows, partners, width):
    row_index = (partners[:, :, None] * width + jnp.arange(width, dtype=jnp.int32)).reshape(-1)
    return jnp.take(held_rows, row_index, axis=0)


def return_rows(pieces, partners, bands):
    flat = pieces.reshape(bands * 2, -1)
    targets = jnp.arange(bands, dtype=jnp.int32)[:, None]
    onehot = (partners.reshape(-1)[None, :] == targets).astype(jnp.float32)
    summed = jnp.dot(onehot, flat, precision=highest)
    width = pieces.shape[0] // (bands * 2)
    return summed.reshape((bands * width,) + pieces.shape[1:])


def body(orbitals, partners, counts):
    bands = lax.axis_size("band")
    slabs = lax.axis_size("slab")
    band_index = lax.axis_index("band")
    slab_index = lax.axis_index("slab")
    orb_group = orbitals.shape[0]
    per_device = orb_group // slabs
    total_orbs = orb_group * bands
    squares = jnp.sum(orbitals * orbitals, axis=0)
    density = 2.0 / total_orbs * lax.psum(squares, "band")
    local_pot = slater_coeff * jnp.cbrt(density)
    band_match = jnp.arange(bands, dtype=jnp.int32)[:, None] == band_index
    my_counts = jnp.sum(jnp.where(band_match, counts, 0), axis=0)
    local_rows = slab_index * per_device + jnp.arange(per_device, dtype=jnp.int32)
    active = (local_rows[None, :] < my_counts[:, None]).astype(jnp.float32)
    own_orbs = lax.all_to_all(orbitals, "slab", split_axis=0, concat_axis=1, tiled=True)
    held_rows = lax.all_to_all(own_orbs, "band", split_axis=1, concat_axis=0, tiled=True)
    wanted = request_rows(held_rows, partners, per_device)
    visitors = lax.all_to_all(wanted, "band", split_axis=0, concat_axis=1, tiled=True)
    visitors = visitors.reshape((2, per_device) + own_orbs.shape[1:])
    own_force, partner_force, energy_term = pair_terms(own_orbs, visitors, active)
    outgoing = partner_force.reshape((2 * per_device,) + own_orbs.shape[1:])
    outgoing = lax.all_to_all(outgoing, "band", split_axis=1, concat_axis=0, tiled=True)
    returned = lax.all_to_all(
        return_rows(outgoing, partners, bands), "band", split_axis=0, concat_axis=1, tiled=True
    )
    exchange_force = lax.all_to_all(
        own_force + returned, "slab", split_axis=1, concat_axis=0, tiled=True
    )
    energy_total = lax.psum(energy_term, ("band", "slab"))
    energy = -energy_total / (2.0 * total_orbs * NX * NY * NZ)
    forces = local_pot[None] * orbitals + exchange_force
    return (forces, energy)


def solution(mesh):
    placed = (P("band", "slab", None), P(), P())
    return jax.shard_map(
        body, mesh=mesh, in_specs=placed, out_specs=(P("band", "slab", None), P()), check_vma=False
    )
```

profile of v0, /device:TPU:0, one launch (start us, length us, event | category | flops | bytes accessed | tf_op | source)
XLA Modules:
  0.0 274.2 jit_solution(14773051680028650991)
XLA Ops:
  7.2 1.9 copy.93
  9.1 4.3 %all-to-all-start = ((f32[4,12,2304]{2,1,0:T(8,128)}), f32[4,12,2304]{2,1,0:T(8,128)S(1)}, u32[]{:S(2)}, u32[]{:S(2)}) async-start(f32[4,12,2304]{2,1,0:T(8,128)} %copy.93), calls=%async_computation | async-start | bytes 1179648 | tf_op jit(solution)/shard_map/all_to_all | solution.py:106
  15.6 7.3 %all-to-all-done = f32[4,12,2304]{2,1,0:T(8,128)S(1)} async-done(((f32[4,12,2304]{2,1,0:T(8,128)}), f32[4,12,2304]{2,1,0:T(8,128)S(1)}, u32[]{:S(2)}, u32[]{:S(2)}) %all-to-all-start) | async-done | bytes 442400 | tf_op jit(solution)/shard_map/all_to_all | solution.py:106
  22.9 1.2 all_to_all.72
  24.1 6.5 %all-to-all-start.1 = ((f32[1,48,2304]{2,0,1:T(1,128)}), f32[1,48,2304]{2,0,1:T(1,128)S(1)}, u32[]{:S(2)}, u32[]{:S(2)}) async-start(f32[1,48,2304]{2,0,1:T(1,128)} %all_to_all.72), calls=%async_computation.1 | async-start | bytes 884736 | tf_op jit(solution)/shard_map/all_to_all | solution.py:107
  32.1 10.9 %all-to-all-done.1 = f32[1,48,2304]{2,0,1:T(1,128)S(1)} async-done(((f32[1,48,2304]{2,0,1:T(1,128)}), f32[1,48,2304]{2,0,1:T(1,128)S(1)}, u32[]{:S(2)}, u32[]{:S(2)}) %all-to-all-start.1) | async-done | bytes 442400 | tf_op jit(solution)/shard_map/all_to_all | solution.py:107
  44.8 1.2 broadcast_select_fusion
  46.0 3.6 %all-to-all-start.2 = ((f32[16,6,2304]{2,1,0:T(8,128)}), f32[16,6,2304]{2,1,0:T(8,128)S(1)}, u32[]{:S(2)}, u32[]{:S(2)}) async-start(f32[16,6,2304]{2,1,0:T(8,128)} %broadcast_select_fusion), calls=%async_computation.2 | async-start | bytes 2359296 | tf_op jit(solution)/shard_map/all_to_all | solution.py:109
  50.4 1.4 add_divide_fusion
  52.5 1.4 copy.119
  54.8 23.2 %all-to-all-done.2 = f32[16,6,2304]{2,1,0:T(8,128)S(1)} async-done(((f32[16,6,2304]{2,1,0:T(8,128)}), f32[16,6,2304]{2,1,0:T(8,128)S(1)}, u32[]{:S(2)}, u32[]{:S(2)}) %all-to-all-start.2) | async-done | bytes 884768 | tf_op jit(solution)/shard_map/all_to_all | solution.py:109
  78.0 1.4 copy.189
  79.4 2.7 reshape.398
  82.1 3.7 %reshape.402 = f32[2,1,48,48,48]{4,3,0,2,1:T(8,128)} reshape(f32[2,8,6,2304]{3,0,2,1:T(2,128)} %bitcast.150) | data formatting | bytes 1769472 | tf_op jit(solution)/shard_map/reshape | solution.py:110
  85.8 3.0 %fusion.19 = f32[2,48,48,96]{3,2,1,0:T(8,128)S(1)} fusion(f32[2,48,48,48]{3,2,0,1:T(8,128)S(1)} %reshape.398, f32[2]{0:T(128)S(1)} %compare_convert_fusion, f32[48,48,48]{2,1,0:T(8,128)S(1)} %mul.404, f32[1,2,48,96]{3,2,0,1:T(8,128)} %get-tuple-element.21, f32[1,2,48,96]{3,2,0,1:T(8,128)} %get-tuple-element.20), kind=kOutput, calls=%fused_computation.23 | convolution fusion | flops 510068736 | bytes 3170312 | tf_op jit(solution)/shard_map/coxyz,cdzk->doxyk/dot_general | solution.py:39
  88.8 2.2 fusion.22
  91.1 2.7 bitcast_multiply_fusion
  93.8 2.2 fusion.27
  96.1 2.7 fusion.30
  98.8 3.2 %copy.111 = f32[2,1,48,48,48]{3,4,2,0,1:T(8,128)} copy(f32[2,1,48,48,48]{4,3,0,2,1:T(8,128)} %reshape.402) | data formatting | bytes 1769472 | tf_op jit(solution)/shard_map/reshape | solution.py:110
  101.9 8.6 %multiply_reduce_fusion = (f32[]{:T(128)}, f32[48,48,48]{1,2,0:T(8,128)}, f32[2,1,48,48,48]{3,4,2,0,1:T(8,128)}) fusion(f32[2,1,48,48,48]{3,4,2,0,1:T(8,128)} %copy.111, f32[2]{0:T(128)S(1)} %compare_convert_fusion, f32[48,48,48]{1,2,0:T(8,128)S(1)} %copy-done, f32[2,48,48,96]{3,2,1,0:T(8,128)S(1)} %fusion.30, f32[1,2,96,48]{2,3,0,1:T(8,128)} %get-tuple-element.17, ...), kind=kOutput, calls=%fused_computation.19 | convolution fusion | flops 510842880 | bytes 4497420 | tf_op jit(solution)/shard_map/coxyk,cdkz->doxyz/dot_general | solution.py:61
  110.5 2.0 copy.113
  112.5 1.1 reshape.403
  113.6 1.1 broadcast_multiply_fusion.1
  115.3 26.3 %all_to_all.79 = f32[2,48,2304]{2,0,1:T(2,128)S(1)} all-to-all(f32[2,48,2304]{2,0,1:T(2,128)S(1)} %copy.114), channel_id=1, replica_groups=mesh['band'=8,'slab'=4] {'band'}, dimensions={1} | all-to-all | bytes 1769472 | tf_op jit(solution)/shard_map/all_to_all | solution.py:113
  143.4 3.5 %all-to-all-start.4 = ((f32[8,6,2304]{2,1,0:T(8,128)}), f32[8,6,2304]{2,1,0:T(8,128)S(1)}, u32[]{:S(2)}, u32[]{:S(2)}) async-start(f32[8,6,2304]{2,1,0:T(8,128)} %copy.117), calls=%async_computation.4 | async-start | bytes 1179648 | tf_op jit(solution)/shard_map/all_to_all | solution.py:114
  149.0 13.9 %all-to-all-done.4 = f32[8,6,2304]{2,1,0:T(8,128)S(1)} async-done(((f32[8,6,2304]{2,1,0:T(8,128)}), f32[8,6,2304]{2,1,0:T(8,128)S(1)}, u32[]{:S(2)}, u32[]{:S(2)}) %all-to-all-start.4) | async-done | bytes 442400 | tf_op jit(solution)/shard_map/all_to_all | solution.py:114
  163.0 1.2 copy.118
  164.2 3.5 %all-to-all-start.5 = ((f32[1,48,2304]{2,0,1:T(1,128)}), f32[1,48,2304]{2,0,1:T(1,128)S(1)}, u32[]{:S(2)}, u32[]{:S(2)}) async-start(f32[1,48,2304]{2,0,1:T(1,128)} %copy.118), calls=%async_computation.5 | async-start | bytes 884736 | tf_op jit(solution)/shard_map/all_to_all | solution.py:117
  167.7 54.9 %all-reduce.2.cloned.1.call-done = f32[12,2304]{1,0:T(8,128)} async-done(((f32[12,2304]{1,0:T(8,128)}), f32[12,2304]{1,0:T(8,128)}) %all-reduce.2.cloned.1.call-update) | async-done | bytes 110608 | tf_op jit(solution)/shard_map/psum | solution.py:100
  223.6 39.6 %psum.15 = f32[]{:T(128)} all-reduce(f32[]{:T(128)} %get-tuple-element.10), channel_id=1, replica_groups=mesh['band'=8,'slab'=4] {'band','slab'}, use_global_device_ids=true, to_apply=%region_5.6 | all-reduce | flops 1 | bytes 8 | tf_op jit(solution)/shard_map/psum | solution.py:120
  265.1 1.0 copy.121
  (60 shorter events, 14.7 us)
Async XLA Ops:
  9.1 13.8 %all-to-all-start = ((f32[4,12,2304]{2,1,0:T(8,128)}), f32[4,12,2304]{2,1,0:T(8,128)S(1)}, u32[]{:S(2)}, u32[]{:S(2)}) async-start(f32[4,12,2304]{2,1,0:T(8,128)} %copy.93), calls=%async_computation | async-start | bytes 1179648 | tf_op jit(solution)/shard_map/all_to_all | solution.py:106
  24.1 18.9 %all-to-all-start.1 = ((f32[1,48,2304]{2,0,1:T(1,128)}), f32[1,48,2304]{2,0,1:T(1,128)S(1)}, u32[]{:S(2)}, u32[]{:S(2)}) async-start(f32[1,48,2304]{2,0,1:T(1,128)} %all_to_all.72), calls=%async_computation.1 | async-start | bytes 884736 | tf_op jit(solution)/shard_map/all_to_all | solution.py:107
  46.0 32.0 %all-to-all-start.2 = ((f32[16,6,2304]{2,1,0:T(8,128)}), f32[16,6,2304]{2,1,0:T(8,128)S(1)}, u32[]{:S(2)}, u32[]{:S(2)}) async-start(f32[16,6,2304]{2,1,0:T(8,128)} %broadcast_select_fusion), calls=%async_computation.2 | async-start | bytes 2359296 | tf_op jit(solution)/shard_map/all_to_all | solution.py:109
  85.7 3.1 %copy-start.6 = (f32[1,2,48,48]{2,3,0,1:T(8,128)S(1)}, f32[1,2,48,48]{2,3,0,1:T(8,128)}, u32[]{:S(2)}) copy-start(f32[1,2,48,48]{2,3,0,1:T(8,128)} %get-tuple-element.13) | copy-start | bytes 55300
  85.8 3.1 %copy-start.7 = (f32[1,2,48,48]{2,3,0,1:T(8,128)S(1)}, f32[1,2,48,48]{2,3,0,1:T(8,128)}, u32[]{:S(2)}) copy-start(f32[1,2,48,48]{2,3,0,1:T(8,128)} %get-tuple-element.18) | copy-start | bytes 55300
  88.8 2.2 copy-start.2
  91.1 2.8 %copy-start.4 = (f32[1,2,48,48]{2,3,1,0:T(8,128)S(1)}, f32[1,2,48,48]{2,3,1,0:T(8,128)}, u32[]{:S(2)}) copy-start(f32[1,2,48,48]{2,3,1,0:T(8,128)} %get-tuple-element.12) | copy-start | bytes 55300
  91.1 2.8 %copy-start.5 = (f32[1,2,48,48]{2,3,1,0:T(8,128)S(1)}, f32[1,2,48,48]{2,3,1,0:T(8,128)}, u32[]{:S(2)}) copy-start(f32[1,2,48,48]{2,3,1,0:T(8,128)} %get-tuple-element.19) | copy-start | bytes 55300
  98.7 3.2 %copy-start = (f32[48,48,48]{1,2,0:T(8,128)S(1)}, f32[48,48,48]{1,2,0:T(8,128)}, u32[]{:S(2)}) copy-start(f32[48,48,48]{1,2,0:T(8,128)} %copy.119) | copy-start | bytes 1327108
  141.6 5.4 %copy-start.3 = (f32[4,12,2304]{2,0,1:T(4,128)S(1)}, f32[4,12,2304]{2,0,1:T(4,128)}, u32[]{:S(2)}) copy-start(f32[4,12,2304]{2,0,1:T(4,128)} %param.3) | copy-start | bytes 1327108
  141.8 6.2 %copy-start.1 = (f32[48,48,48]{1,2,0:T(8,128)S(1)}, f32[48,48,48]{1,2,0:T(8,128)}, u32[]{:S(2)}) copy-start(f32[48,48,48]{1,2,0:T(8,128)} %get-tuple-element.11) | copy-start | bytes 1327108
  143.4 19.5 %all-to-all-start.4 = ((f32[8,6,2304]{2,1,0:T(8,128)}), f32[8,6,2304]{2,1,0:T(8,128)S(1)}, u32[]{:S(2)}, u32[]{:S(2)}) async-start(f32[8,6,2304]{2,1,0:T(8,128)} %copy.117), calls=%async_computation.4 | async-start | bytes 1179648 | tf_op jit(solution)/shard_map/all_to_all | solution.py:114
  147.0 75.6 %all-reduce.2.cloned.1.call-start = ((), (), s32[]{:S(2)}) async-start(), calls=%async_computation.6 | async-start | bytes 294912 | tf_op jit(solution)/shard_map/psum | solution.py:100
  164.2 99.7 %all-to-all-start.5 = ((f32[1,48,2304]{2,0,1:T(1,128)}), f32[1,48,2304]{2,0,1:T(1,128)S(1)}, u32[]{:S(2)}, u32[]{:S(2)}) async-start(f32[1,48,2304]{2,0,1:T(1,128)} %copy.118), calls=%async_computation.5 | async-start | bytes 884736 | tf_op jit(solution)/shard_map/all_to_all | solution.py:117
Sparse Core Ops, SparseCore 0:
  151.1 71.4 all-reduce.1
where the time goes:
time: 275 us; the launch traced here: 274 us
  waiting for transfers between devices  110 us (40%)
  blocking collectives  65.9 us (24%)
  local copies, waits for them, and re-layouts  26.8 us (10%)
  matrix products  22.1 us (8%)
  starting transfers between devices  21.4 us (8%)
  between operations  16.1 us (6%)
  other arithmetic  11.6 us (4%)
    psum x1, waiting for transfers between devices, body(): density = 2.0 / total_orbs * lax.psum(squares, 'band')  54.9 us
    psum x1, blocking collectives, body(): energy_total = lax.psum(energy_term, ('band', 'slab'))  39.6 us
    all_to_all x1, blocking collectives, body(): lax.all_to_all(outgoing, 'band', split_axis=1, concat_axis=0, tiled=True)  26.3 us
    all_to_all x1, waiting for transfers between devices, body(): lax.all_to_all(wanted, 'band', split_axis=0, concat_axis=1, tiled=True)  23.2 us
    all_to_all x1, waiting for transfers between devices, body(): lax.all_to_all(return_rows(outgoing, partners, bands), 'band', split_axis...  13.9 us
    all_to_all x1, waiting for transfers between devices, body(): lax.all_to_all(own_orbs, 'band', split_axis=1, concat_axis=0, tiled=True)  10.9 us
    reshape x3, local copies, waits for them, and re-layouts, body(): visitors = visitors.reshape((2, per_device) + own_orbs.shape[1:])  9.54 us
    dot_general x1, matrix products, screened_potential(): jnp.einsum('coxyk,cdkz->doxyz', spectrum, dft_block(NZP, NZ, NZP, -1.0),...  8.55 us
  transfers between devices with their start and end apart: 6, of which 5 were waited for; matrix products, arithmetic and copies ran while one was open for 5% of the time, Pallas kernels for 0%

commit v1 on v0

--- a/solution.py
+++ b/solution.py
@@ -88,6 +88,19 @@
     return summed.reshape((bands * width,) + pieces.shape[1:])
 
 
+def band_sum(value, bands):
+    reach = 1
+    while reach < bands:
+        value = value + lax.ppermute(value, "band", [(i, i ^ reach) for i in range(bands)])
+        reach *= 2
+    return value
+
+
+def total_of(value, devices):
+    sent = jnp.broadcast_to(value, (devices, 1, 128))
+    return jnp.sum(lax.all_to_all(sent, ("band", "slab"), 0, 0)[:, 0, 0])
+
+
 def body(orbitals, partners, counts):
     bands = lax.axis_size("band")
     slabs = lax.axis_size("slab")
@@ -97,7 +110,7 @@
     per_device = orb_group // slabs
     total_orbs = orb_group * bands
     squares = jnp.sum(orbitals * orbitals, axis=0)
-    density = 2.0 / total_orbs * lax.psum(squares, "band")
+    density = 2.0 / total_orbs * band_sum(squares, bands)
     local_pot = slater_coeff * jnp.cbrt(density)
     band_match = jnp.arange(bands, dtype=jnp.int32)[:, None] == band_index
     my_counts = jnp.sum(jnp.where(band_match, counts, 0), axis=0)
@@ -117,7 +130,7 @@
     exchange_force = lax.all_to_all(
         own_force + returned, "slab", split_axis=1, concat_axis=0, tiled=True
     )
-    energy_total = lax.psum(energy_term, ("band", "slab"))
+    energy_total = total_of(energy_term, bands * slabs)
     energy = -energy_total / (2.0 * total_orbs * NX * NY * NZ)
     forces = local_pot[None] * orbitals + exchange_force
     return (forces, energy)

time: 275 us -> 188 us (0.68)
  waiting for transfers between devices: 110 us -> 65.4 us
  blocking collectives: 65.9 us -> 26.3 us
  between operations: 16.1 us -> 2.78 us
  starting transfers between devices: 21.4 us -> 29 us
    psum x1 -> x0, waiting for transfers between devices: 54.9 us -> none  [body(): density = 2.0 / total_orbs * lax.psum(squares, 'band')]
    psum x1 -> x0, blocking collectives: 39.6 us -> none  [body(): energy_total = lax.psum(energy_term, ('band', 'slab'))]
    all_to_all x1, waiting for transfers between devices: 13.9 us -> 0.01 us  [body(): lax.all_to_all(return_rows(outgoing, partners, bands), 'band', split_axis...]
    ppermute x0 -> x3, waiting for transfers between devices: none -> 13.9 us  [band_sum(): lax.ppermute(value, 'band', [(i, i ^ reach) for i in range(bands)])]
    all_to_all x1, waiting for transfers between devices: 0.01 us -> 5.48 us  [body(): lax.all_to_all(own_force + returned, 'slab', split_axis=1, concat_axis=0,...]
    all_to_all x0 -> x1, waiting for transfers between devices: none -> 4.66 us  [total_of(): return jnp.sum(lax.all_to_all(sent, ('band', 'slab'), 0, 0)[:, 0, 0])]
    ppermute x0 -> x3, starting transfers between devices: none -> 4.13 us  [band_sum(): lax.ppermute(value, 'band', [(i, i ^ reach) for i in range(bands)])]
    all_to_all x0 -> x1, starting transfers between devices: none -> 3.47 us  [total_of(): return jnp.sum(lax.all_to_all(sent, ('band', 'slab'), 0, 0)[:, 0, 0])]
  transfers between devices with their start and end apart: 6 -> 9, of which waited for: 5 -> 7; matrix products, arithmetic and copies ran while one was open for 5% -> 8% of each run, Pallas kernels for 0% -> 0%
where the time goes in v1:
time: 188 us; the launch traced here: 187 us
  waiting for transfers between devices  65.4 us (35%)
  local copies, waits for them, and re-layouts  29 us (15%)
  starting transfers between devices  29 us (15%)
  blocking collectives  26.3 us (14%)
  matrix products  21.6 us (11%)
  other arithmetic  12.7 us (7%)
  between operations  2.78 us (1%)
    all_to_all x1, blocking collectives, body(): lax.all_to_all(outgoing, 'band', split_axis=1, concat_axis=0, tiled=True)  26.3 us
    all_to_all x1, waiting for transfers between devices, body(): lax.all_to_all(wanted, 'band', split_axis=0, concat_axis=1, tiled=True)  23.2 us
    ppermute x3, waiting for transfers between devices, band_sum(): lax.ppermute(value, 'band', [(i, i ^ reach) for i in range(bands)])  13.9 us
    all_to_all x1, waiting for transfers between devices, body(): lax.all_to_all(own_orbs, 'band', split_axis=1, concat_axis=0, tiled=True)  10.9 us
    reshape x3, local copies, waits for them, and re-layouts, body(): visitors = visitors.reshape((2, per_device) + own_orbs.shape[1:])  9.43 us
    dot_general x1, matrix products, screened_potential(): jnp.einsum('coxyk,cdkz->doxyz', spectrum, dft_block(NZP, NZ, NZP, -1.0),...  8.13 us
    all_to_all x1, waiting for transfers between devices, body(): lax.all_to_all(orbitals, 'slab', split_axis=0, concat_axis=1, tiled=True)  7.28 us
    all_to_all x1, starting transfers between devices, body(): lax.all_to_all(own_orbs, 'band', split_axis=1, concat_axis=0, tiled=True)  6.47 us
  transfers between devices with their start and end apart: 9, of which 7 were waited for; matrix products, arithmetic and copies ran while one was open for 8% of the time, Pallas kernels for 0%

profile of v1, /device:TPU:0, one launch (start us, length us, event | category | flops | bytes accessed | tf_op | source)
XLA Modules:
  0.0 186.7 jit_solution(14183099838319847257)
XLA Ops:
  0.6 1.9 %copy.151 = f32[4,12,2304]{2,1,0:T(8,128)} copy(f32[4,12,2304]{2,0,1:T(4,128)} %param.3) | data formatting | bytes 884736 | tf_op args[0]
  2.5 4.3 %all-to-all-start = ((f32[4,12,2304]{2,1,0:T(8,128)}), f32[4,12,2304]{2,1,0:T(8,128)S(1)}, u32[]{:S(2)}, u32[]{:S(2)}) async-start(f32[4,12,2304]{2,1,0:T(8,128)} %copy.151), calls=%async_computation | async-start | bytes 1179648 | tf_op jit(solution)/shard_map/all_to_all | solution.py:119
  9.0 7.3 %all-to-all-done = f32[4,12,2304]{2,1,0:T(8,128)S(1)} async-done(((f32[4,12,2304]{2,1,0:T(8,128)}), f32[4,12,2304]{2,1,0:T(8,128)S(1)}, u32[]{:S(2)}, u32[]{:S(2)}) %all-to-all-start) | async-done | bytes 442400 | tf_op jit(solution)/shard_map/all_to_all | solution.py:119
  17.5 6.5 %all-to-all-start.1 = ((f32[1,48,2304]{2,0,1:T(1,128)}), f32[1,48,2304]{2,0,1:T(1,128)S(1)}, u32[]{:S(2)}, u32[]{:S(2)}) async-start(f32[1,48,2304]{2,0,1:T(1,128)} %all_to_all.76), calls=%async_computation.1 | async-start | bytes 884736 | tf_op jit(solution)/shard_map/all_to_all | solution.py:120
  25.6 10.9 %all-to-all-done.1 = f32[1,48,2304]{2,0,1:T(1,128)S(1)} async-done(((f32[1,48,2304]{2,0,1:T(1,128)}), f32[1,48,2304]{2,0,1:T(1,128)S(1)}, u32[]{:S(2)}, u32[]{:S(2)}) %all-to-all-start.1) | async-done | bytes 442400 | tf_op jit(solution)/shard_map/all_to_all | solution.py:120
  39.4 3.6 %all-to-all-start.2 = ((f32[16,6,2304]{2,1,0:T(8,128)}), f32[16,6,2304]{2,1,0:T(8,128)S(1)}, u32[]{:S(2)}, u32[]{:S(2)}) async-start(f32[16,6,2304]{2,1,0:T(8,128)} %broadcast_select_fusion), calls=%async_computation.2 | async-start | bytes 2359296 | tf_op jit(solution)/shard_map/all_to_all | solution.py:122
  43.8 1.4 add_divide_fusion
  46.0 1.4 copy.177
  48.3 23.2 %all-to-all-done.2 = f32[16,6,2304]{2,1,0:T(8,128)S(1)} async-done(((f32[16,6,2304]{2,1,0:T(8,128)}), f32[16,6,2304]{2,1,0:T(8,128)S(1)}, u32[]{:S(2)}, u32[]{:S(2)}) %all-to-all-start.2) | async-done | bytes 884768 | tf_op jit(solution)/shard_map/all_to_all | solution.py:122
  71.4 1.4 copy.249
  72.8 2.7 %reshape.398 = f32[2,48,48,48]{3,2,0,1:T(8,128)S(1)} reshape(f32[2,8,6,2304]{3,0,2,1:T(2,128)} %bitcast.149) | data formatting | bytes 1769472 | tf_op jit(solution)/shard_map/reshape | solution.py:123
  75.6 3.6 %reshape.402 = f32[2,1,48,48,48]{4,3,0,2,1:T(8,128)} reshape(f32[2,8,6,2304]{3,0,2,1:T(2,128)} %bitcast.150) | data formatting | bytes 1769472 | tf_op jit(solution)/shard_map/reshape | solution.py:123
  79.2 3.0 %fusion.19 = f32[2,48,48,96]{3,2,1,0:T(8,128)S(1)} fusion(f32[2,48,48,48]{3,2,0,1:T(8,128)S(1)} %reshape.398, f32[2]{0:T(128)S(1)} %compare_convert_fusion, f32[48,48,48]{2,1,0:T(8,128)S(1)} %mul.404, f32[1,2,48,96]{3,2,0,1:T(8,128)} %get-tuple-element.25, f32[1,2,48,96]{3,2,0,1:T(8,128)} %get-tuple-element.24), kind=kOutput, calls=%fused_computation.23 | convolution fusion | flops 510068736 | bytes 3170312 | tf_op jit(solution)/shard_map/coxyz,cdzk->doxyk/dot_general | solution.py:39
  82.3 2.2 %fusion.22 = f32[2,48,48,96]{3,2,1,0:T(8,128)S(1)} fusion(f32[2,48,48,96]{3,2,1,0:T(8,128)S(1)} %fusion.19, f32[1,2,48,48]{2,3,0,1:T(8,128)S(1)} %copy-done.7, f32[1,2,48,48]{2,3,0,1:T(8,128)S(1)} %copy-done.8), kind=kOutput, calls=%fused_computation.24 | convolution fusion | flops 509617152 | bytes 3575808 | tf_op jit(solution)/shard_map/coxyk,cdyq->doxqk/dot_general | solution.py:42
  84.5 2.7 %bitcast_multiply_fusion = f32[2,48,48,96]{3,1,2,0:T(8,128)S(1)} fusion(f32[2,48,48,96]{3,2,1,0:T(8,128)S(1)} %fusion.22, f32[48,48,96]{2,0,1:T(8,128)S(1)} %copy-done, f32[1,2,48,48]{2,3,0,1:T(8,128)S(1)} %copy-done.7, f32[1,2,48,48]{2,3,0,1:T(8,128)S(1)} %copy-done.8), kind=kOutput, calls=%fused_computation.7 | convolution fusion | flops 510059520 | bytes 4460544 | tf_op jit(solution)/shard_map/coxqk,cdxp->dopqk/dot_general | solution.py:45
  87.3 2.2 %fusion.27 = f32[2,48,48,96]{3,1,2,0:T(8,128)S(1)} fusion(f32[2,48,48,96]{3,1,2,0:T(8,128)S(1)} %bitcast_multiply_fusion, f32[1,2,48,48]{2,3,1,0:T(8,128)S(1)} %copy-done.6, f32[1,2,48,48]{2,3,1,0:T(8,128)S(1)} %copy-done.5), kind=kOutput, calls=%fused_computation.25 | convolution fusion | flops 509617152 | bytes 3575808 | tf_op jit(solution)/shard_map/copqk,cdpx->doxqk/dot_general | solution.py:55
  89.5 2.7 %fusion.30 = f32[2,48,48,96]{3,2,1,0:T(8,128)S(1)} fusion(f32[2,48,48,96]{3,1,2,0:T(8,128)S(1)} %fusion.27, f32[1,2,48,48]{2,3,1,0:T(8,128)S(1)} %copy-done.6, f32[1,2,48,48]{2,3,1,0:T(8,128)S(1)} %copy-done.5), kind=kOutput, calls=%fused_computation.26 | convolution fusion | flops 509617152 | bytes 3575808 | tf_op jit(solution)/shard_map/coxqk,cdqy->doxyk/dot_general | solution.py:58
  92.2 3.1 %copy.169 = f32[2,1,48,48,48]{3,4,2,0,1:T(8,128)} copy(f32[2,1,48,48,48]{4,3,0,2,1:T(8,128)} %reshape.402) | data formatting | bytes 1769472 | tf_op jit(solution)/shard_map/reshape | solution.py:123
  95.2 8.1 %multiply_reduce_fusion = (f32[]{:T(128)}, f32[48,48,48]{1,2,0:T(8,128)S(1)}, f32[2,1,48,48,48]{3,4,2,0,1:T(8,128)}) fusion(f32[2,1,48,48,48]{3,4,2,0,1:T(8,128)} %copy.169, f32[2]{0:T(128)S(1)} %compare_convert_fusion, f32[48,48,48]{1,2,0:T(8,128)} %copy.177, f32[2,48,48,96]{3,2,1,0:T(8,128)S(1)} %fusion.30, f32[1,2,96,48]{2,3,0,1:T(8,128)} %get-tuple-element.21, ...), kind=kOutput, calls=%fused_computation.19 | convolution fusion | flops 510842880 | bytes 4497420 | tf_op jit(solution)/shard_map/coxyk,cdkz->doxyz/dot_general | solution.py:61
  103.4 2.0 %copy.171 = f32[2,1,48,48,48]{4,3,2,0,1:T(8,128)S(1)} copy(f32[2,1,48,48,48]{3,4,2,0,1:T(8,128)} %get-tuple-element.26) | data formatting | bytes 1769472 | tf_op jit(solution)/shard_map/coxyk,cdkz->doxyz/transpose | solution.py:61
  105.4 1.9 %reshape.403 = f32[2,48,2304]{2,1,0:T(8,128)} reshape(f32[2,1,48,48,48]{4,3,2,0,1:T(8,128)S(1)} %copy.171) | data formatting | bytes 1769472 | tf_op jit(solution)/shard_map/reshape | solution.py:70
  107.3 1.4 broadcast_multiply_fusion.1
  109.4 26.3 %all_to_all.84 = f32[2,48,2304]{2,0,1:T(2,128)S(1)} all-to-all(f32[2,48,2304]{2,0,1:T(2,128)S(1)} %copy.172), channel_id=1, replica_groups=mesh['band'=8,'slab'=4] {'band'}, dimensions={1} | all-to-all | bytes 1769472 | tf_op jit(solution)/shard_map/all_to_all | solution.py:126
  137.5 3.5 %all-to-all-start.4 = ((f32[8,6,2304]{2,1,0:T(8,128)}), f32[8,6,2304]{2,1,0:T(8,128)S(1)}, u32[]{:S(2)}, u32[]{:S(2)}) async-start(f32[8,6,2304]{2,1,0:T(8,128)} %copy.175), calls=%async_computation.4 | async-start | bytes 1179648 | tf_op jit(solution)/shard_map/all_to_all | solution.py:127
  141.3 2.0 %collective-permute-start = (f32[12,2304]{1,0:T(8,128)S(1)}, f32[12,2304]{1,0:T(8,128)S(1)}, u32[]{:S(2)}, u32[]{:S(2)}) collective-permute-start(f32[12,2304]{1,0:T(8,128)S(1)} %multiply_reduce_fusion.2), channel_id=1, source_target_pairs={{0,4},{4,0},{8,12},{12,8},{16,20},{20,16},{24,28},{28,24},{1,5},{5... | collective-permute-start | bytes 331784 | tf_op jit(solution)/shard_map/ppermute | solution.py:94
  143.3 8.1 %collective-permute-done = f32[12,2304]{1,0:T(8,128)S(1)} collective-permute-done((f32[12,2304]{1,0:T(8,128)S(1)}, f32[12,2304]{1,0:T(8,128)S(1)}, u32[]{:S(2)}, u32[]{:S(2)}) %collective-permute-start) | collective-permute-done | bytes 110624 | tf_op jit(solution)/shard_map/ppermute | solution.py:94
  152.1 5.8 %collective-permute-done.1 = f32[12,2304]{1,0:T(8,128)S(1)} collective-permute-done((f32[12,2304]{1,0:T(8,128)S(1)}, f32[12,2304]{1,0:T(8,128)S(1)}, u32[]{:S(2)}, u32[]{:S(2)}) %collective-permute-start.1) | collective-permute-done | bytes 110624 | tf_op jit(solution)/shard_map/ppermute | solution.py:94
  158.6 1.4 collective-permute-start.2
  161.3 3.5 %all-to-all-start.6 = ((f32[32,1,128]{2,1,0:T(1,128)}), f32[32,1,128]{2,1,0:T(1,128)S(1)}, u32[]{:S(2)}, u32[]{:S(2)}) async-start(f32[32,1,128]{2,1,0:T(1,128)} %broadcast_in_dim.40), calls=%async_computation.6 | async-start | bytes 32768 | tf_op jit(solution)/shard_map/all_to_all | solution.py:101
  167.2 4.7 %all-to-all-done.6 = f32[32,1,128]{2,1,0:T(1,128)S(1)} async-done(((f32[32,1,128]{2,1,0:T(1,128)}), f32[32,1,128]{2,1,0:T(1,128)S(1)}, u32[]{:S(2)}, u32[]{:S(2)}) %all-to-all-start.6) | async-done | bytes 16416 | tf_op jit(solution)/shard_map/all_to_all | solution.py:101
  171.9 3.5 %all-to-all-start.5 = ((f32[1,48,2304]{2,0,1:T(1,128)}), f32[1,48,2304]{2,0,1:T(1,128)S(1)}, u32[]{:S(2)}, u32[]{:S(2)}) async-start(f32[1,48,2304]{2,0,1:T(1,128)} %copy.176), calls=%async_computation.5 | async-start | bytes 884736 | tf_op jit(solution)/shard_map/all_to_all | solution.py:130
  177.8 5.5 %all-to-all-done.5 = f32[1,48,2304]{2,0,1:T(1,128)S(1)} async-done(((f32[1,48,2304]{2,0,1:T(1,128)}), f32[1,48,2304]{2,0,1:T(1,128)S(1)}, u32[]{:S(2)}, u32[]{:S(2)}) %all-to-all-start.5) | async-done | bytes 442400 | tf_op jit(solution)/shard_map/all_to_all | solution.py:130
  (70 shorter events, 22.2 us)
Async XLA Ops:
  2.5 13.8 %all-to-all-start = ((f32[4,12,2304]{2,1,0:T(8,128)}), f32[4,12,2304]{2,1,0:T(8,128)S(1)}, u32[]{:S(2)}, u32[]{:S(2)}) async-start(f32[4,12,2304]{2,1,0:T(8,128)} %copy.151), calls=%async_computation | async-start | bytes 1179648 | tf_op jit(solution)/shard_map/all_to_all | solution.py:119
  17.5 18.9 %all-to-all-start.1 = ((f32[1,48,2304]{2,0,1:T(1,128)}), f32[1,48,2304]{2,0,1:T(1,128)S(1)}, u32[]{:S(2)}, u32[]{:S(2)}) async-start(f32[1,48,2304]{2,0,1:T(1,128)} %all_to_all.76), calls=%async_computation.1 | async-start | bytes 884736 | tf_op jit(solution)/shard_map/all_to_all | solution.py:120
  39.4 32.0 %all-to-all-start.2 = ((f32[16,6,2304]{2,1,0:T(8,128)}), f32[16,6,2304]{2,1,0:T(8,128)S(1)}, u32[]{:S(2)}, u32[]{:S(2)}) async-start(f32[16,6,2304]{2,1,0:T(8,128)} %broadcast_select_fusion), calls=%async_computation.2 | async-start | bytes 2359296 | tf_op jit(solution)/shard_map/all_to_all | solution.py:122
  79.2 3.1 %copy-start.7 = (f32[1,2,48,48]{2,3,0,1:T(8,128)S(1)}, f32[1,2,48,48]{2,3,0,1:T(8,128)}, u32[]{:S(2)}) copy-start(f32[1,2,48,48]{2,3,0,1:T(8,128)} %get-tuple-element.17) | copy-start | bytes 55300
  79.2 3.1 %copy-start.8 = (f32[1,2,48,48]{2,3,0,1:T(8,128)S(1)}, f32[1,2,48,48]{2,3,0,1:T(8,128)}, u32[]{:S(2)}) copy-start(f32[1,2,48,48]{2,3,0,1:T(8,128)} %get-tuple-element.22) | copy-start | bytes 55300
  82.3 2.2 %copy-start = (f32[48,48,96]{2,0,1:T(8,128)S(1)}, f32[48,48,96]{2,0,1:T(8,128)}, u32[]{:S(2)}) copy-start(f32[48,48,96]{2,0,1:T(8,128)} %add_divide_fusion) | copy-start | bytes 2654212
  84.5 2.8 %copy-start.5 = (f32[1,2,48,48]{2,3,1,0:T(8,128)S(1)}, f32[1,2,48,48]{2,3,1,0:T(8,128)}, u32[]{:S(2)}) copy-start(f32[1,2,48,48]{2,3,1,0:T(8,128)} %get-tuple-element.16) | copy-start | bytes 55300
  84.5 2.8 %copy-start.6 = (f32[1,2,48,48]{2,3,1,0:T(8,128)S(1)}, f32[1,2,48,48]{2,3,1,0:T(8,128)}, u32[]{:S(2)}) copy-start(f32[1,2,48,48]{2,3,1,0:T(8,128)} %get-tuple-element.23) | copy-start | bytes 55300
  135.7 5.3 %copy-start.1 = (f32[4,12,2304]{2,0,1:T(4,128)S(1)}, f32[4,12,2304]{2,0,1:T(4,128)}, u32[]{:S(2)}) copy-start(f32[4,12,2304]{2,0,1:T(4,128)} %param.3) | copy-start | bytes 1327108
  137.5 22.5 %all-to-all-start.4 = ((f32[8,6,2304]{2,1,0:T(8,128)}), f32[8,6,2304]{2,1,0:T(8,128)S(1)}, u32[]{:S(2)}, u32[]{:S(2)}) async-start(f32[8,6,2304]{2,1,0:T(8,128)} %copy.175), calls=%async_computation.4 | async-start | bytes 1179648 | tf_op jit(solution)/shard_map/all_to_all | solution.py:127
  141.3 10.0 %collective-permute-start = (f32[12,2304]{1,0:T(8,128)S(1)}, f32[12,2304]{1,0:T(8,128)S(1)}, u32[]{:S(2)}, u32[]{:S(2)}) collective-permute-start(f32[12,2304]{1,0:T(8,128)S(1)} %multiply_reduce_fusion.2), channel_id=1, source_target_pairs={{0,4},{4,0},{8,12},{12,8},{16,20},{20,16},{24,28},{28,24},{1,5},{5... | collective-permute-start | bytes 331784 | tf_op jit(solution)/shard_map/ppermute | solution.py:94
  151.3 6.6 %collective-permute-start.1 = (f32[12,2304]{1,0:T(8,128)S(1)}, f32[12,2304]{1,0:T(8,128)S(1)}, u32[]{:S(2)}, u32[]{:S(2)}) collective-permute-start(f32[12,2304]{1,0:T(8,128)S(1)} %add.192), channel_id=1, source_target_pairs={{0,8},{4,12},{8,0},{12,4},{16,24},{20,28},{24,16},{28,20},{1,9},{5... | collective-permute-start | bytes 331784 | tf_op jit(solution)/shard_map/ppermute | solution.py:94
  158.6 16.7 %collective-permute-start.2 = (f32[12,2304]{1,0:T(8,128)}, f32[12,2304]{1,0:T(8,128)}, u32[]{:S(2)}, u32[]{:S(2)}) collective-permute-start(f32[12,2304]{1,0:T(8,128)} %add.193), channel_id=1, source_target_pairs={{0,16},{4,20},{8,24},{12,28},{16,0},{20,4},{24,8},{28,12},{1,17},{... | collective-permute-start | bytes 331784 | tf_op jit(solution)/shard_map/ppermute | solution.py:94
  160.0 4.7 %copy-start.3 = (f32[8,6,2304]{2,1,0:T(8,128)}, f32[8,6,2304]{2,1,0:T(8,128)S(1)}, u32[]{:S(2)}) copy-start(f32[8,6,2304]{2,1,0:T(8,128)S(1)} %all-to-all-done.4) | copy-start | bytes 1327108
  161.3 10.7 %all-to-all-start.6 = ((f32[32,1,128]{2,1,0:T(1,128)}), f32[32,1,128]{2,1,0:T(1,128)S(1)}, u32[]{:S(2)}, u32[]{:S(2)}) async-start(f32[32,1,128]{2,1,0:T(1,128)} %broadcast_in_dim.40), calls=%async_computation.6 | async-start | bytes 32768 | tf_op jit(solution)/shard_map/all_to_all | solution.py:101
  164.8 1.1 copy-start.4
  166.0 18.4 %copy-start.2 = (f32[4,12,2304]{2,0,1:T(4,128)S(1)}, f32[4,12,2304]{2,0,1:T(4,128)}, u32[]{:S(2)}) copy-start(f32[4,12,2304]{2,0,1:T(4,128)} %param.3) | copy-start | bytes 1327108
  171.9 11.4 %all-to-all-start.5 = ((f32[1,48,2304]{2,0,1:T(1,128)}), f32[1,48,2304]{2,0,1:T(1,128)S(1)}, u32[]{:S(2)}, u32[]{:S(2)}) async-start(f32[1,48,2304]{2,0,1:T(1,128)} %copy.176), calls=%async_computation.5 | async-start | bytes 884736 | tf_op jit(solution)/shard_map/all_to_all | solution.py:130
